TPU v7x, 256 devices: a whole 4x4x8 slice. The times are simulated.
256 devices in a mesh: req: 16 (over y_hi, z), head: 16 (over y_lo, x, core).
Axes of the slice: x: 4, y: 4 (y_hi: 2, y_lo: 2; y = y_hi * 2 + y_lo), z: 8, core: 2. Of those that a mesh axis runs over, the one named last changes fastest.
Arguments:
- queries: bfloat16 [4096, 8192], P('req', 'head'), may hold values from -8 to 8
- new_keys: bfloat16 [4096, 1024], P('req'), may hold values from -5 to 5
- new_values: bfloat16 [4096, 1024], P('req'), may hold values from -24 to 24
- cache_keys: bfloat16 [32, 256, 1024], P('req'), may hold values from -4 to 4
- cache_values: bfloat16 [32, 256, 1024], P('req'), may hold values from -24 to 24
- request_slot: int32 [16], P('req'), may hold values from 0 to 1
- tenant_ids: int32 [4096], P('req'), may hold values from 0 to 255
- out_weight: bfloat16 [8192, 8192], P('req', 'head'), may hold values from -0.0625 to 0.0625
- adapter_down: bfloat16 [8192, 8192], P('head', 'req'), may hold values from -0.0625 to 0.0625
- adapter_up: bfloat16 [8192, 8192], P('req', 'head'), may hold values from -1 to 1
Outputs:
- mixed: bfloat16 [4096, 8192], P('req', 'head')
All inputs are finite; a program needn't handle non-finite values.
Results may differ from a plain program's by a relative error of at most 0.0064.
Values may be sent and summed in bfloat16 or wider, within the bound.
No kernel may reach another device: no remote copies, remote signals or barrier semaphores. Data moves between devices by JAX's collectives and lax.ppermute only.
A program may use at most 128 MiB of HBM per device.

v0:
```python
import jax
import jax.numpy as jnp
from jax import lax
from jax.sharding import PartitionSpec as P

HEADS = 64
HD = 128
KVH = 8
RANK = 32


def pick_heads(block, shared_index):
    spread = block.reshape(block.shape[0], KVH, HD)
    return jnp.take(spread, shared_index, axis=1)


def select(tenants, count):
    return tenants[:, None] == jnp.arange(count, dtype=jnp.int32)[None, :]


def shrink(block, tenants, weights):
    count = weights.shape[1] // RANK
    product = jnp.dot(block, weights, preferred_element_type=jnp.float32)
    product = product.reshape(block.shape[0], count, RANK)
    chosen = select(tenants, count).astype(jnp.float32)
    return jnp.sum(product * chosen[:, :, None], axis=1)


def expand(shrunk, tenants, weights):
    count = weights.shape[0] // RANK
    chosen = select(tenants, count).astype(jnp.bfloat16)
    spread = (chosen[:, :, None] * shrunk[:, None, :]).reshape(shrunk.shape[0], count * RANK)
    return jnp.dot(spread, weights, preferred_element_type=jnp.float32)


def attention(queries, new_keys, new_values, cache_keys, cache_values, request_slot):
    row_count = queries.shape[0]
    local_heads = queries.shape[1] // HD
    group = HEADS // KVH
    shared_index = (
        lax.axis_index("head") * local_heads + jnp.arange(local_heads, dtype=jnp.int32)
    ) // group
    slot_index = request_slot[0]
    keys_old = pick_heads(
        lax.dynamic_index_in_dim(cache_keys, slot_index, 0, keepdims=False), shared_index
    )
    values_old = pick_heads(
        lax.dynamic_index_in_dim(cache_values, slot_index, 0, keepdims=False), shared_index
    )
    keys_new = pick_heads(new_keys, shared_index)
    values_new = pick_heads(new_values, shared_index)
    split_queries = queries.reshape(row_count, local_heads, HD)
    scale = HD ** (-0.5)
    scores_old = (
        jnp.einsum("qhd,khd->hqk", split_queries, keys_old, preferred_element_type=jnp.float32)
        * scale
    )
    scores_new = (
        jnp.einsum("qhd,khd->hqk", split_queries, keys_new, preferred_element_type=jnp.float32)
        * scale
    )
    causal = (
        jnp.arange(row_count, dtype=jnp.int32)[:, None]
        >= jnp.arange(row_count, dtype=jnp.int32)[None, :]
    )
    scores_new = jnp.where(causal[None], scores_new, -1e30)
    highest = jnp.maximum(jnp.max(scores_old, axis=2), jnp.max(scores_new, axis=2))[:, :, None]
    weights_old = jnp.exp(scores_old - highest)
    weights_new = jnp.where(causal[None], jnp.exp(scores_new - highest), 0.0)
    total = jnp.sum(weights_old, axis=2, keepdims=True) + jnp.sum(
        weights_new, axis=2, keepdims=True
    )
    probs_old = (weights_old / total).astype(jnp.bfloat16)
    probs_new = (weights_new / total).astype(jnp.bfloat16)
    output = jnp.einsum("hqk,khd->qhd", probs_old, values_old, preferred_element_type=jnp.float32)
    output = output + jnp.einsum(
        "hqk,khd->qhd", probs_new, values_new, preferred_element_type=jnp.float32
    )
    return output.reshape(row_count, local_heads * HD).astype(jnp.bfloat16)


def local(
    queries,
    new_keys,
    new_values,
    cache_keys,
    cache_values,
    request_slot,
    tenant_ids,
    out_weight,
    adapter_down,
    adapter_up,
):
    attended = attention(queries, new_keys, new_values, cache_keys, cache_values, request_slot)
    partial_value = shrink(
        attended, tenant_ids, lax.all_gather(adapter_down, "req", axis=1, tiled=True)
    )
    shrunk = lax.psum(partial_value, "head").astype(jnp.bfloat16)
    columns = lax.all_gather(out_weight, "req", axis=0, tiled=True)
    rows_block = lax.all_to_all(columns, "head", split_axis=0, concat_axis=1, tiled=True)
    base_term = jnp.dot(attended, rows_block, preferred_element_type=jnp.float32)
    base = lax.psum_scatter(base_term, "head", scatter_dimension=1, tiled=True)
    summed = expand(shrunk, tenant_ids, lax.all_gather(adapter_up, "req", axis=0, tiled=True))
    delta = lax.optimization_barrier(summed.astype(jnp.bfloat16)).astype(jnp.float32)
    return (base + delta).astype(jnp.bfloat16)


def solution(mesh):
    placed = (
        P("req", "head"),
        P("req", None),
        P("req", None),
        P("req", None, None),
        P("req", None, None),
        P("req"),
        P("req"),
        P("req", "head"),
        P("head", "req"),
        P("req", "head"),
    )
    return jax.shard_map(
        local, mesh=mesh, in_specs=placed, out_specs=P("req", "head"), check_vma=False
    )
```

profile of v0, /device:TPU:16, one launch (start us, length us, event | category | flops | bytes accessed | tf_op | source)
XLA Modules:
  0.0 553.8 jit_solution(7732991442768242154)
XLA Ops:
  6.5 0.7 all-gather.4.cloned.1.call-update
  7.3 2.1 copy.41
  9.5 0.7 all-gather.8.cloned.1.call-update
  10.1 135.3 %all-gather.4.cloned.1.call-done = bf16[8192,512]{1,0:T(8,128)(2,1)} async-done(((bf16[512,512]{1,0:T(8,128)(2,1)}), bf16[8192,512]{1,0:T(8,128)(2,1)}) %all-gather.4.cloned.1.call-update) | async-done | bytes 8388624 | tf_op jit(solution)/shard_map/all_gather | solution.py:99
  145.4 6.1 %all-to-all-start = ((bf16[16,512,512]{2,1,0:T(8,128)(2,1)}), bf16[16,512,512]{2,1,0:T(8,128)(2,1)}, u32[]{:S(2)}, u32[]{:S(2)}) async-start(bf16[16,512,512]{2,1,0:T(8,128)(2,1)} %bitcast.65), calls=%async_computation | async-start | bytes 16777216 | tf_op jit(solution)/shard_map/all_to_all | solution.py:100
  152.3 1.1 constant_dynamic-slice_fusion
  154.4 0.6 gather_fusion.1
  155.0 0.6 gather_fusion.2
  156.1 0.6 gather_fusion
  157.2 0.6 gather_fusion.3
  159.0 0.4 fusion.13
  159.4 0.5 fusion.7
  159.9 104.5 %all-to-all-done = bf16[16,512,512]{2,1,0:T(8,128)(2,1)} async-done(((bf16[16,512,512]{2,1,0:T(8,128)(2,1)}), bf16[16,512,512]{2,1,0:T(8,128)(2,1)}, u32[]{:S(2)}, u32[]{:S(2)}) %all-to-all-start) | async-done | bytes 8388640 | tf_op jit(solution)/shard_map/all_to_all | solution.py:100
  264.4 12.3 %copy.40 = bf16[512,16,512]{0,2,1:T(8,128)(2,1)} copy(bf16[512,16,512]{2,0,1:T(8,128)(2,1)} %bitcast.14) | data formatting | bytes 16777216 | tf_op jit(solution)/shard_map/all_to_all | solution.py:100
  276.8 9.0 %fusion.44 = f32[256,8192]{1,0:T(8,128)} fusion(bf16[256,512]{0,1:T(8,128)(2,1)S(1)} %bitcast.70, bf16[512,8192]{0,1:T(8,128)(2,1)} %bitcast.63), kind=kOutput, calls=%fused_computation.68 | convolution fusion | flops 2147483648 | bytes 17039360 | tf_op jit(solution)/shard_map/dot_general | solution.py:101
  285.8 0.7 copy-done.5
  286.5 40.1 %all-gather.6.cloned.1.call-done = bf16[512,8192]{0,1:T(8,128)(2,1)} async-done(((bf16[512,512]{0,1:T(8,128)(2,1)}), bf16[512,8192]{0,1:T(8,128)(2,1)}) %all-gather.6.cloned.1.call-update) | async-done | bytes 8388624 | tf_op jit(solution)/shard_map/all_gather | solution.py:96
  326.6 12.9 %multiply_reduce_fusion = f32[256,32]{0,1:T(8,128)S(1)} fusion(f32[256,256]{0,1:T(8,128)S(1)} %get-tuple-element.9, bf16[256,512,1]{0,1,2:T(8,128)(2,1)S(1)} %bitcast.71, bf16[256,32,512]{2,1,0:T(8,128)(2,1)} %bitcast.72), kind=kOutput, calls=%fused_computation.6 | convolution fusion | flops 2151669760 | bytes 8945664 | tf_op jit(solution)/shard_map/dot_general | solution.py:23
  339.5 58.6 %psum.7 = bf16[256,32]{0,1:T(8,128)(2,1)S(1)} all-reduce(f32[256,32]{0,1:T(8,128)S(1)} %multiply_reduce_fusion), channel_id=1, replica_groups=mesh['req'=16,'head'=16] {'head'}, use_global_device_ids=true, to_apply=%region_6.8 | all-reduce | flops 8192 | bytes 49152 | tf_op jit(solution)/shard_map/psum | solution.py:98
  398.1 2.2 broadcast_multiply_fusion
  400.3 66.4 %all-gather.8.cloned.1.call-done = bf16[8192,512]{1,0:T(8,128)(2,1)} async-done(((bf16[512,512]{1,0:T(8,128)(2,1)}), bf16[8192,512]{1,0:T(8,128)(2,1)}) %all-gather.8.cloned.1.call-update) | async-done | bytes 8388624 | tf_op jit(solution)/shard_map/all_gather | solution.py:103
  466.8 7.0 %convolution_convert_fusion = bf16[256,512]{1,0:T(8,128)(2,1)S(1)} fusion(bf16[256,8192]{0,1:T(8,128)(2,1)} %bitcast.64, bf16[8192,512]{1,0:T(8,128)(2,1)} %all-gather.8.cloned.1.call-done), kind=kOutput, calls=%fused_computation.15 | convolution fusion | flops 2147614720 | bytes 12845056 | tf_op jit(solution)/shard_map/dot_general | solution.py:33
  473.8 71.6 %reduce-scatter.2.cloned.1.call-done = f32[256,512]{1,0:T(8,128)} async-done(((f32[256,8192]{1,0:T(8,128)}), f32[256,512]{1,0:T(8,128)}) %reduce-scatter.2.cloned.1.call-update) | async-done | bytes 524304 | tf_op jit(solution)/shard_map/reduce_scatter | solution.py:102
  545.4 1.8 add_convert_fusion
  (35 shorter events, 3.3 us)
Async XLA Ops:
  6.5 151.3 %copy-start = (bf16[256,512]{1,0:T(8,128)(2,1)S(1)}, bf16[256,512]{1,0:T(8,128)(2,1)}, u32[]{:S(2)}) copy-start(bf16[256,512]{1,0:T(8,128)(2,1)} %param.12) | copy-start | bytes 786436
  6.5 138.9 %all-gather.4.cloned.1.call-start = ((), (), s32[]{:S(2)}) async-start(), calls=%async_computation.2 | async-start | bytes 8912896 | tf_op jit(solution)/shard_map/all_gather | solution.py:99
  7.3 319.3 %all-gather.6.cloned.1.call-start = ((), (), s32[]{:S(2)}) async-start(), calls=%async_computation.4 | async-start | bytes 8912896 | tf_op jit(solution)/shard_map/all_gather | solution.py:96
  9.4 457.3 %all-gather.8.cloned.1.call-start = ((), (), s32[]{:S(2)}) async-start(), calls=%async_computation.5 | async-start | bytes 8912896 | tf_op jit(solution)/shard_map/all_gather | solution.py:103
  145.4 6.8 %copy-start.4 = (bf16[2,256,1024]{2,1,0:T(8,128)(2,1)S(1)}, bf16[2,256,1024]{2,1,0:T(8,128)(2,1)}, u32[]{:S(2)}) copy-start(bf16[2,256,1024]{2,1,0:T(8,128)(2,1)} %param.15) | copy-start | bytes 3145732
  145.4 8.5 %copy-start.2 = (bf16[256,1024]{1,0:T(8,128)(2,1)S(1)}, bf16[256,1024]{1,0:T(8,128)(2,1)}, u32[]{:S(2)}) copy-start(bf16[256,1024]{1,0:T(8,128)(2,1)} %param.13) | copy-start | bytes 1572868
  145.4 119.0 %all-to-all-start = ((bf16[16,512,512]{2,1,0:T(8,128)(2,1)}), bf16[16,512,512]{2,1,0:T(8,128)(2,1)}, u32[]{:S(2)}, u32[]{:S(2)}) async-start(bf16[16,512,512]{2,1,0:T(8,128)(2,1)} %bitcast.65), calls=%async_computation | async-start | bytes 16777216 | tf_op jit(solution)/shard_map/all_to_all | solution.py:100
  151.5 5.2 copy-start.3
  151.5 393.9 %reduce-scatter.2.cloned.1.call-start = ((), (), s32[]{:S(2)}) async-start(), calls=%async_computation.3 | async-start | bytes 8912896 | tf_op jit(solution)/shard_map/reduce_scatter | solution.py:102
  285.8 0.7 copy-start.5
  466.7 80.5 %copy-start.1 = (bf16[256,512]{1,0:T(8,128)(2,1)S(1)}, bf16[256,512]{1,0:T(8,128)(2,1)}, u32[]{:S(2)}) copy-start(bf16[256,512]{1,0:T(8,128)(2,1)} %param.12) | copy-start | bytes 786436
Sparse Core Ops, SparseCore 0:
  9.9 135.4 all-gather.3
  148.0 178.5 all-gather.5
  329.2 137.5 all-gather.7
  469.2 76.2 reduce-scatter.1
where the time goes:
time: 554 us
  waiting for transfers between devices  419 us (76%)
  blocking collectives  58.6 us (11%)
  matrix products  30.6 us (6%)
  local copies, waits for them, and re-layouts  20.5 us (4%)
  between operations  14 us (3%)
  starting transfers between devices  6.19 us (1%)
    all_gather x1, waiting for transfers between devices, local(): columns = lax.all_gather(out_weight, 'req', axis=0, tiled=True)  135 us
    all_to_all x1, waiting for transfers between devices, local(): lax.all_to_all(columns, 'head', split_axis=0, concat_axis=1, tiled=True)  105 us
    reduce_scatter x1, waiting for transfers between devices, local(): base = lax.psum_scatter(base_term, 'head', scatter_dimension=1, tiled=True)  71.6 us
    all_gather x1, waiting for transfers between devices, local(): lax.all_gather(adapter_up, 'req', axis=0, tiled=True)  66.4 us
    psum x1, blocking collectives, local(): shrunk = lax.psum(partial_value, 'head').astype(jnp.bfloat16)  58.6 us
    all_gather x1, waiting for transfers between devices, local(): lax.all_gather(adapter_down, 'req', axis=1, tiled=True)  40.1 us
    dot_general x1, matrix products, shrink(): product = jnp.dot(block, weights, preferred_element_type=jnp.float32)  12.9 us
    all_to_all x1, local copies, waits for them, and re-layouts, local(): lax.all_to_all(columns, 'head', split_axis=0, concat_axis=1, tiled=True)  12.3 us
  transfers between devices with their start and end apart: 5, of which 5 were waited for; matrix products, arithmetic and copies ran while one was open for 10% of the time, Pallas kernels for 0%

commit v1 on v0

--- a/solution.py
+++ b/solution.py
@@ -96,7 +96,9 @@
         attended, tenant_ids, lax.all_gather(adapter_down, "req", axis=1, tiled=True)
     )
     shrunk = lax.psum(partial_value, "head").astype(jnp.bfloat16)
-    columns = lax.all_gather(out_weight, "req", axis=0, tiled=True)
+    columns = jnp.concatenate(
+        lax.all_to_all(jnp.stack([out_weight] * lax.axis_size("req")), "req", 0, 0), axis=0
+    )
     rows_block = lax.all_to_all(columns, "head", split_axis=0, concat_axis=1, tiled=True)
     base_term = jnp.dot(attended, rows_block, preferred_element_type=jnp.float32)
     base = lax.psum_scatter(base_term, "head", scatter_dimension=1, tiled=True)

time: 554 us -> 532 us (0.960)
  waiting for transfers between devices: 419 us -> 391 us
  starting transfers between devices: 6.19 us -> 16.3 us
  local copies, waits for them, and re-layouts: 20.5 us -> 13.5 us
    all_to_all x0 -> x1, waiting for transfers between devices: none -> 218 us  [local(): lax.all_to_all(jnp.stack([out_weight] * lax.axis_size('req')), 'req', 0, 0)]
    all_gather x1 -> x0, waiting for transfers between devices: 135 us -> none  [local(): columns = lax.all_gather(out_weight, 'req', axis=0, tiled=True)]
    reduce_scatter x1, waiting for transfers between devices: 71.6 us -> 0.03 us  [local(): base = lax.psum_scatter(base_term, 'head', scatter_dimension=1, tiled=True)]
    all_gather x1, waiting for transfers between devices: 40.1 us -> 0.02 us  [local(): lax.all_gather(adapter_down, 'req', axis=1, tiled=True)]
    all_to_all x1 -> x0, local copies, waits for them, and re-layouts: 12.3 us -> none  [local(): lax.all_to_all(columns, 'head', split_axis=0, concat_axis=1, tiled=True)]
    all_to_all x0 -> x1, starting transfers between devices: none -> 11.4 us  [local(): lax.all_to_all(jnp.stack([out_weight] * lax.axis_size('req')), 'req', 0, 0)]
  transfers between devices with their start and end apart: 5 -> 5, of which waited for: 5 -> 3; matrix products, arithmetic and copies ran while one was open for 10% -> 8% of each run, Pallas kernels for 0% -> 0%
where the time goes in v1:
time: 532 us; the launch traced here: 528 us
  waiting for transfers between devices  391 us (73%)
  blocking collectives  56.5 us (11%)
  matrix products  30.6 us (6%)
  starting transfers between devices  16.3 us (3%)
  between operations  15.8 us (3%)
  local copies, waits for them, and re-layouts  13.5 us (3%)
    all_to_all x1, waiting for transfers between devices, local(): lax.all_to_all(jnp.stack([out_weight] * lax.axis_size('req')), 'req', 0, 0)  218 us
    all_to_all x1, waiting for transfers between devices, local(): lax.all_to_all(columns, 'head', split_axis=0, concat_axis=1, tiled=True)  104 us
    all_gather x1, waiting for transfers between devices, local(): lax.all_gather(adapter_up, 'req', axis=0, tiled=True)  68.4 us
    psum x1, blocking collectives, local(): shrunk = lax.psum(partial_value, 'head').astype(jnp.bfloat16)  56.5 us
    dot_general x1, matrix products, shrink(): product = jnp.dot(block, weights, preferred_element_type=jnp.float32)  12.9 us
    all_to_all x1, starting transfers between devices, local(): lax.all_to_all(jnp.stack([out_weight] * lax.axis_size('req')), 'req', 0, 0)  11.4 us
  transfers between devices with their start and end apart: 5, of which 3 were waited for; matrix products, arithmetic and copies ran while one was open for 8% of the time, Pallas kernels for 0%

profile of v1, /device:TPU:16, one launch (start us, length us, event | category | flops | bytes accessed | tf_op | source)
XLA Modules:
  0.0 528.3 jit_solution(11038765103236102470)
XLA Ops:
  7.4 2.1 copy.42
  9.5 1.3 copy.41
  10.8 4.0 stack.2
  14.8 11.4 %all-to-all-start = ((bf16[16,512,512]{1,2,0:T(8,128)(2,1)}), bf16[16,512,512]{1,2,0:T(8,128)(2,1)}, u32[]{:S(2)}, u32[]{:S(2)}) async-start(bf16[16,512,512]{1,2,0:T(8,128)(2,1)} %stack.2), calls=%async_computation | async-start | bytes 16777216 | tf_op jit(solution)/shard_map/all_to_all | solution.py:100
  26.3 0.7 all-gather.5.cloned.1.call-update
  27.0 217.7 %all-to-all-done = bf16[16,512,512]{1,2,0:T(8,128)(2,1)} async-done(((bf16[16,512,512]{1,2,0:T(8,128)(2,1)}), bf16[16,512,512]{1,2,0:T(8,128)(2,1)}, u32[]{:S(2)}, u32[]{:S(2)}) %all-to-all-start) | async-done | bytes 8388640 | tf_op jit(solution)/shard_map/all_to_all | solution.py:100
  244.7 4.8 all-to-all-start.1
  250.3 1.1 constant_dynamic-slice_fusion
  252.4 0.6 gather_fusion.1
  253.0 0.6 gather_fusion.2
  254.1 0.6 gather_fusion
  255.2 0.6 gather_fusion.3
  256.2 0.4 fusion.43
  257.0 0.4 fusion.13
  257.4 0.5 fusion.7
  257.9 104.3 %all-to-all-done.1 = bf16[16,512,512]{1,2,0:T(8,128)(2,1)} async-done(((bf16[16,512,512]{1,2,0:T(8,128)(2,1)}), bf16[16,512,512]{1,2,0:T(8,128)(2,1)}, u32[]{:S(2)}, u32[]{:S(2)}) %all-to-all-start.1) | async-done | bytes 8388640 | tf_op jit(solution)/shard_map/all_to_all | solution.py:102
  362.2 9.0 %fusion.44 = f32[256,8192]{1,0:T(8,128)} fusion(bf16[256,512]{0,1:T(8,128)(2,1)S(1)} %bitcast.68, bf16[512,8192]{0,1:T(8,128)(2,1)} %bitcast.14), kind=kOutput, calls=%fused_computation.68 | convolution fusion | flops 2147483648 | bytes 17039360 | tf_op jit(solution)/shard_map/dot_general | solution.py:103
  371.2 0.7 copy-done.5
  371.9 12.9 %multiply_reduce_fusion = f32[256,32]{0,1:T(8,128)S(1)} fusion(f32[256,256]{0,1:T(8,128)S(1)} %get-tuple-element.9, bf16[256,512,1]{0,1,2:T(8,128)(2,1)S(1)} %bitcast.69, bf16[256,32,512]{2,1,0:T(8,128)(2,1)} %bitcast.70), kind=kOutput, calls=%fused_computation.6 | convolution fusion | flops 2151669760 | bytes 8945664 | tf_op jit(solution)/shard_map/dot_general | solution.py:23
  384.9 56.5 %psum.7 = bf16[256,32]{0,1:T(8,128)(2,1)S(1)} all-reduce(f32[256,32]{0,1:T(8,128)S(1)} %multiply_reduce_fusion), channel_id=1, replica_groups=mesh['req'=16,'head'=16] {'head'}, use_global_device_ids=true, to_apply=%region_6.8 | all-reduce | flops 8192 | bytes 49152 | tf_op jit(solution)/shard_map/psum | solution.py:98
  441.4 2.2 broadcast_multiply_fusion
  443.6 68.4 %all-gather.5.cloned.1.call-done = bf16[8192,512]{1,0:T(8,128)(2,1)} async-done(((bf16[512,512]{1,0:T(8,128)(2,1)}), bf16[8192,512]{1,0:T(8,128)(2,1)}) %all-gather.5.cloned.1.call-update) | async-done | bytes 8388624 | tf_op jit(solution)/shard_map/all_gather | solution.py:105
  512.0 7.0 %convolution_convert_fusion = bf16[256,512]{1,0:T(8,128)(2,1)S(1)} fusion(bf16[256,8192]{0,1:T(8,128)(2,1)} %bitcast.63, bf16[8192,512]{1,0:T(8,128)(2,1)} %all-gather.5.cloned.1.call-done), kind=kOutput, calls=%fused_computation.15 | convolution fusion | flops 2147614720 | bytes 12845056 | tf_op jit(solution)/shard_map/dot_general | solution.py:33
  519.1 1.8 add_convert_fusion
  (35 shorter events, 2.9 us)
Async XLA Ops:
  7.4 248.5 %copy-start = (bf16[256,512]{1,0:T(8,128)(2,1)S(1)}, bf16[256,512]{1,0:T(8,128)(2,1)}, u32[]{:S(2)}) copy-start(bf16[256,512]{1,0:T(8,128)(2,1)} %param.12) | copy-start | bytes 786436
  7.4 364.6 %all-gather.3.cloned.1.call-start = ((), (), s32[]{:S(2)}) async-start(), calls=%async_computation.4 | async-start | bytes 8912896 | tf_op jit(solution)/shard_map/all_gather | solution.py:96
  14.8 229.9 %all-to-all-start = ((bf16[16,512,512]{1,2,0:T(8,128)(2,1)}), bf16[16,512,512]{1,2,0:T(8,128)(2,1)}, u32[]{:S(2)}, u32[]{:S(2)}) async-start(bf16[16,512,512]{1,2,0:T(8,128)(2,1)} %stack.2), calls=%async_computation | async-start | bytes 16777216 | tf_op jit(solution)/shard_map/all_to_all | solution.py:100
  26.2 485.8 %all-gather.5.cloned.1.call-start = ((), (), s32[]{:S(2)}) async-start(), calls=%async_computation.5 | async-start | bytes 8912896 | tf_op jit(solution)/shard_map/all_gather | solution.py:105
  27.0 223.3 %copy-start.4 = (bf16[2,256,1024]{2,1,0:T(8,128)(2,1)S(1)}, bf16[2,256,1024]{2,1,0:T(8,128)(2,1)}, u32[]{:S(2)}) copy-start(bf16[2,256,1024]{2,1,0:T(8,128)(2,1)} %param.15) | copy-start | bytes 3145732
  27.0 224.9 %copy-start.2 = (bf16[256,1024]{1,0:T(8,128)(2,1)S(1)}, bf16[256,1024]{1,0:T(8,128)(2,1)}, u32[]{:S(2)}) copy-start(bf16[256,1024]{1,0:T(8,128)(2,1)} %param.13) | copy-start | bytes 1572868
  244.7 117.5 %all-to-all-start.1 = ((bf16[16,512,512]{1,2,0:T(8,128)(2,1)}), bf16[16,512,512]{1,2,0:T(8,128)(2,1)}, u32[]{:S(2)}, u32[]{:S(2)}) async-start(bf16[16,512,512]{1,2,0:T(8,128)(2,1)} %all-to-all-done), calls=%async_computation.1 | async-start | bytes 16777216 | tf_op jit(solution)/shard_map/all_to_all | solution.py:102
  249.5 5.2 copy-start.3
  249.5 269.6 %reduce-scatter.2.cloned.1.call-start = ((), (), s32[]{:S(2)}) async-start(), calls=%async_computation.3 | async-start | bytes 8912896 | tf_op jit(solution)/shard_map/reduce_scatter | solution.py:104
  371.2 0.7 copy-start.5
  512.0 8.9 %copy-start.1 = (bf16[256,512]{1,0:T(8,128)(2,1)S(1)}, bf16[256,512]{1,0:T(8,128)(2,1)}, u32[]{:S(2)}) copy-start(bf16[256,512]{1,0:T(8,128)(2,1)} %param.12) | copy-start | bytes 786436
Sparse Core Ops, SparseCore 0:
  10.8 299.6 all-gather.2
  313.0 198.9 all-gather.4
Sparse Core Ops, SparseCore 1:
  371.3 84.1 reduce-scatter.1
